TPU v7x, 256 devices: a whole 4x4x8 slice. The times are simulated.
256 devices in a mesh: section: 8 (over x, core), fsdp: 16 (over y_hi, z), dp: 2 (over y_lo).
Axes of the slice: x: 4, y: 4 (y_hi: 2, y_lo: 2; y = y_hi * 2 + y_lo), z: 8, core: 2. Of those that a mesh axis runs over, the one named last changes fastest.
Arguments:
- section_inputs: bfloat16 [8, 2, 2048, 4096], P('section', 'dp', 'fsdp'), may hold values from -6 to 6
- queries: bfloat16 [8, 2, 2048, 4096], P('section', 'dp', 'fsdp'), may hold values from -110 to 110
- keys: bfloat16 [8, 2, 2048, 1024], P('section', 'dp', 'fsdp'), may hold values from -4.5 to 4.5
- w_value: bfloat16 [8, 4096, 1024], P('section', 'fsdp'), may hold values from -0.09375 to 0.09375
- gain: bfloat16 [8, 4096], P('section', 'fsdp'), may hold values from 0.5 to 1.5
- section_grads_in: bfloat16 [8, 2, 2048, 4096], P('section', 'dp', 'fsdp'), may hold values from -6 to 6
Outputs:
- passed_grads: bfloat16 [8, 2, 2048, 4096], P('section', 'dp', 'fsdp')
- w_value_grad: bfloat16 [8, 4096, 1024], P('section', ('fsdp', 'dp'))
- gain_grad: float32 [8, 4096], P('section', ('fsdp', 'dp'))
All inputs are finite; a program needn't handle non-finite values.
Results may differ from a plain program's by a relative error of at most 0.029.
Values may be sent and summed in bfloat16 or wider, within the bound.
A program may use at most 64 MiB of HBM per device.

v0:
```python
import jax
import jax.numpy as jnp
from jax import lax
from jax.sharding import PartitionSpec as P

KVH = 8
DH = 128
MEM = 128
GROUP = 4


NEG_FILL = -1e30
EPSILON = 1e-05


def from_behind(block, axis, distance):
    devices = range(lax.axis_size(axis))
    route = [((i - distance) % len(devices), i) for i in devices]
    return lax.ppermute(block, axis, route)


def per_device(section_inputs, queries, keys, w_value, gain, section_grads_in):
    tok_rows = section_inputs.shape[2]
    kv_width = keys.shape[3]
    kv_heads = KVH
    group_size = GROUP
    head_dim = DH
    score_scale = head_dim ** (-0.5)
    my_slot = lax.axis_index("fsdp")
    inputs = section_inputs[0, 0].astype(jnp.float32)
    inv_rms = lax.rsqrt(jnp.mean(inputs * inputs, axis=1, keepdims=True) + EPSILON)
    normed = inputs * inv_rms
    all_keys = lax.all_gather(keys[0, 0], "fsdp", axis=0, tiled=True)
    full_weight, gain_full = (
        lax.all_gather(w_value[0], "fsdp", axis=0, tiled=True),
        lax.all_gather(gain[0], "fsdp", axis=0, tiled=True),
    )
    total_rows = all_keys.shape[0]
    query_pos = my_slot * tok_rows + jnp.arange(tok_rows, dtype=jnp.int32)
    key_pos = jnp.arange(total_rows, dtype=jnp.int32)
    visible = (key_pos[None, :] <= query_pos[:, None]) | (key_pos[None, :] < MEM)
    query_groups = (
        queries[0, 0].reshape(tok_rows, kv_heads, group_size, head_dim).transpose(1, 2, 0, 3)
    )
    key_groups = all_keys.reshape(total_rows, kv_heads, head_dim).transpose(1, 0, 2)
    cotangent = section_grads_in[0, 0]
    grad_groups = cotangent.reshape(tok_rows, kv_heads, group_size, head_dim).transpose(1, 0, 2, 3)

    def group_values(operands):
        query_group, key_group, grad_group = operands
        scores = (
            jnp.einsum("htd,kd->htk", query_group, key_group, preferred_element_type=jnp.float32)
            * score_scale
        )
        scores = jnp.where(visible[None], scores, NEG_FILL)
        row_top = jnp.max(scores, axis=2, keepdims=True)
        weights_exp = jnp.exp(scores - row_top)
        attn_probs = (weights_exp / jnp.sum(weights_exp, axis=2, keepdims=True)).astype(
            jnp.bfloat16
        )
        return jnp.einsum("htk,thd->kd", attn_probs, grad_group, preferred_element_type=jnp.float32)

    partial_values = lax.map(group_values, (query_groups, key_groups, grad_groups))
    partial_values = partial_values.transpose(1, 0, 2).reshape(total_rows, kv_width)
    value_grad = lax.psum_scatter(
        partial_values.astype(jnp.bfloat16), "fsdp", scatter_dimension=0, tiled=True
    )
    gain_float = gain_full.astype(jnp.float32)
    normed_b = (normed * gain_float).astype(jnp.bfloat16)
    normed_grad = lax.dot_general(
        value_grad, full_weight, (((1,), (1,)), ((), ())), preferred_element_type=jnp.float32
    )
    scaled = normed_grad * gain_float
    inner_mean = jnp.mean(scaled * normed, axis=1, keepdims=True)
    input_grad = (cotangent.astype(jnp.float32) + inv_rms * (scaled - normed * inner_mean)).astype(
        jnp.bfloat16
    )
    passed = from_behind(input_grad, "section", -1)
    gain_part = jnp.sum(normed_grad * normed, axis=0)
    weight_part = lax.dot_general(
        normed_b, value_grad, (((0,), (0,)), ((), ())), preferred_element_type=jnp.float32
    )
    weight_shard, gain_shard = (
        lax.psum_scatter(
            weight_part.astype(jnp.bfloat16), ("fsdp", "dp"), scatter_dimension=0, tiled=True
        ).astype(jnp.float32),
        lax.psum_scatter(
            gain_part.astype(jnp.bfloat16), ("fsdp", "dp"), scatter_dimension=0, tiled=True
        ).astype(jnp.float32),
    )
    return (passed[None, None], weight_shard.astype(jnp.bfloat16)[None], gain_shard[None])


def solution(mesh):
    return jax.shard_map(
        per_device,
        mesh=mesh,
        in_specs=(
            P("section", "dp", "fsdp", None),
            P("section", "dp", "fsdp", None),
            P("section", "dp", "fsdp", None),
            P("section", "fsdp", None),
            P("section", "fsdp"),
            P("section", "dp", "fsdp", None),
        ),
        out_specs=(
            P("section", "dp", "fsdp", None),
            P("section", ("fsdp", "dp"), None),
            P("section", ("fsdp", "dp")),
        ),
        check_vma=False,
    )
```

profile of v0, /device:TPU:1, one launch (start us, length us, event | category | flops | bytes accessed | tf_op | source)
XLA Modules:
  0.0 723.8 jit_solution(3587904438740722615)
XLA Ops:
  12.4 103.9 %all-gather.6.cloned.1.call-done = bf16[1,1,2048,1024]{2,3,1,0:T(8,128)(2,1)} async-done(((bf16[1,1,128,1024]{2,3,1,0:T(8,128)(2,1)}), bf16[1,1,2048,1024]{2,3,1,0:T(8,128)(2,1)}) %all-gather.6.cloned.1.call-update) | async-done | bytes 4194320 | tf_op jit(solution)/shard_map/all_gather | solution.py:33
  116.3 55.6 %while.11 = (s32[]{:T(128)}, bf16[8,2048,128]{1,2,0:T(8,128)(2,1)}, bf16[8,4,128,128]{2,3,1,0:T(8,128)(2,1)S(1)}, bf16[8,2048,128]{1,2,0:T(8,128)(2,1)}, bf16[8,...) while((s32[]{:T(128)}, bf16[8,2048,128]{1,2,0:T(8,128)(2,1)}, ...), condition=%wide.region_4.5_spmd.clone, body=%wide.region_1.4_spmd.clone.sunk | while | flops 815272448 | bytes 3286613 | solution.py:63
  116.5 2.8 fusion.88
  119.4 3.9 fusion.89
  126.3 3.9 fusion.89
  133.3 3.9 fusion.89
  137.4 2.8 fusion.88
  140.2 3.9 fusion.89
  144.4 2.8 fusion.88
  147.2 3.9 fusion.89
  151.3 2.8 fusion.88
  154.1 3.9 fusion.89
  158.3 2.8 fusion.88
  161.1 3.9 fusion.89
  165.2 2.8 fusion.88
  168.0 3.9 fusion.89
  172.0 6.4 copy.27
  179.2 29.5 %all-gather.2 = bf16[1,4096]{1,0:T(2,128)(2,1)S(1)} all-gather(bf16[1,256]{1,0:T(2,128)(2,1)S(1)} %copy-done.3), channel_id=4, replica_groups=mesh['section'=8,'fsdp'=16,'dp'=2] {'fsdp'}, dimensions={1}, use_global_device_ids=true | all-gather | bytes 8704 | tf_op jit(solution)/shard_map/all_gather | solution.py:36
  209.0 176.2 %reduce-scatter.7.cloned.1.call-done = bf16[128,1024]{1,0:T(8,128)(2,1)} async-done(((bf16[2048,1024]{1,0:T(8,128)(2,1)}), bf16[128,1024]{1,0:T(8,128)(2,1)}) %reduce-scatter.7.cloned.1.call-update) | async-done | bytes 262160
  385.2 6.6 convolution_convert_fusion
  391.9 132.5 %all-gather.8.cloned.1.call-done = bf16[1,4096,1024]{2,1,0:T(8,128)(2,1)} async-done(((bf16[1,256,1024]{2,1,0:T(8,128)(2,1)}), bf16[1,4096,1024]{2,1,0:T(8,128)(2,1)}) %all-gather.8.cloned.1.call-update) | async-done | bytes 8388624 | tf_op jit(solution)/shard_map/all_gather | solution.py:35
  524.3 6.5 fusion.61
  534.2 62.6 %all-reduce = bf16[4096]{0:T(1024)(128)(2,1)S(1)} all-reduce(bf16[4096]{0:T(1024)(128)(2,1)S(1)} %get-tuple-element.68), channel_id=7, replica_groups=mesh['section'=8,'fsdp'=16,'dp'=2] {'fsdp','dp'}, use_global_device_ids=true, to_apply=%region_9.10.clone | all-reduce | flops 4096 | bytes 16384
  597.4 118.9 %reduce-scatter.5.cloned.1.call-done = bf16[128,1024]{1,0:T(8,128)(2,1)} async-done(((bf16[4096,1024]{1,0:T(8,128)(2,1)}), bf16[128,1024]{1,0:T(8,128)(2,1)}) %reduce-scatter.5.cloned.1.call-update) | async-done | bytes 262160 | tf_op jit(solution)/shard_map/reduce_scatter | solution.py:84
  (44 shorter events, 18.0 us)
Async XLA Ops:
  7.2 109.1 %all-gather.6.cloned.1.call-start = ((), (), s32[]{:S(2)}) async-start(), calls=%async_computation.3 | async-start | bytes 4456448 | tf_op jit(solution)/shard_map/all_gather | solution.py:33
  9.0 376.2 %reduce-scatter.7.cloned.1.call-start = ((), (), s32[]{:S(2)}) async-start(), calls=%async_computation.5 | async-start | bytes 4456448
  178.3 0.8 copy-start.3
  178.3 30.3 %copy-start = (bf16[1,1,128,4096]{3,2,1,0:T(8,128)(2,1)S(1)}, bf16[1,1,128,4096]{3,2,1,0:T(8,128)(2,1)}, u32[]{:S(2)}) copy-start(bf16[1,1,128,4096]{3,2,1,0:T(8,128)(2,1)} %param.8) | copy-start | bytes 3145732
  178.4 345.9 %all-gather.8.cloned.1.call-start = ((), (), s32[]{:S(2)}) async-start(), calls=%async_computation.4 | async-start | bytes 8912896 | tf_op jit(solution)/shard_map/all_gather | solution.py:35
  179.1 537.2 %reduce-scatter.5.cloned.1.call-start = ((), (), s32[]{:S(2)}) async-start(), calls=%async_computation.2 | async-start | bytes 8650752 | tf_op jit(solution)/shard_map/reduce_scatter | solution.py:84
  391.8 132.5 %copy-start.2 = (bf16[128,1024]{1,0:T(8,128)(2,1)S(1)}, bf16[128,1024]{1,0:T(8,128)(2,1)}, u32[]{:S(2)}) copy-start(bf16[128,1024]{1,0:T(8,128)(2,1)} %reduce-scatter.7.cloned.1.call-done) | copy-start | bytes 786436
  391.8 139.0 %copy-start.1 = (bf16[1,1,128,4096]{3,2,1,0:T(8,128)(2,1)S(1)}, bf16[1,1,128,4096]{3,2,1,0:T(8,128)(2,1)}, u32[]{:S(2)}) copy-start(bf16[1,1,128,4096]{3,2,1,0:T(8,128)(2,1)} %param.13) | copy-start | bytes 3145732
  530.8 2.2 copy-start.4
  531.6 65.9 %collective-permute-start = (bf16[128,4096]{1,0:T(8,128)(2,1)S(1)}, bf16[128,4096]{1,0:T(8,128)(2,1)S(1)}, u32[]{:S(2)}, u32[]{:S(2)}) collective-permute-start(bf16[128,4096]{1,0:T(8,128)(2,1)S(1)} %fusion.59), channel_id=1, source_target_pairs={{32,0},{64,32},{96,64},{128,96},{160,128},{192,160},{224,192},{0,2... | collective-permute-start | bytes 3145736 | tf_op jit(solution)/shard_map/ppermute | solution.py:19
Sparse Core Ops, SparseCore 0:
  11.0 105.2 all-gather.5
  178.5 206.6 reduce-scatter.6
  387.8 136.4 all-gather.7
  527.3 188.9 reduce-scatter.4
where the time goes:
time: 727 us; the launch traced here: 724 us
  waiting for transfers between devices  532 us (73%)
  blocking collectives  92.1 us (13%)
  matrix products  66.8 us (9%)
  between operations  14.5 us (2%)
  local copies, waits for them, and re-layouts  13 us (2%)
    unnamed x5, waiting for transfers between devices  177 us
    all_gather x1, waiting for transfers between devices, per_device(): lax.all_gather(w_value[0], 'fsdp', axis=0, tiled=True)  132 us
    reduce_scatter x1, waiting for transfers between devices, per_device(): lax.psum_scatter(weight_part.astype(jnp.bfloat16), ('fsdp', 'dp'), scatte...  119 us
    all_gather x1, waiting for transfers between devices, per_device(): all_keys = lax.all_gather(keys[0, 0], 'fsdp', axis=0, tiled=True)  104 us
    unnamed x1, blocking collectives  62.6 us
    dot_general x8, matrix products, group_values(): jnp.einsum('htk,thd->kd', attn_probs, grad_group, preferred_element_type=...  31.2 us
    all_gather x1, blocking collectives, per_device(): lax.all_gather(gain[0], 'fsdp', axis=0, tiled=True)  29.5 us
    sub x8, matrix products, group_values(): weights_exp = jnp.exp(scores - row_top)  22.5 us
  transfers between devices with their start and end apart: 5, of which 4 were waited for; matrix products, arithmetic and copies ran while one was open for 3% of the time, Pallas kernels for 0%

commit v1 on v0

v1 whole, which is shorter than its diff:
```python
import functools
import math

import jax
import jax.numpy as jnp
from jax import lax
from jax.experimental import pallas as pl
from jax.experimental.pallas import tpu as pltpu
from jax.sharding import PartitionSpec as P

MESH = pl.DeviceIdType.MESH
BF16, F32 = jnp.bfloat16, jnp.float32

NY = 4
NZ = 8
TOK = 128
D = 4096
KV = 1024
DH = 128
GROUP = 4
QC = D // NY
KC = KV // NY
GL = KC // DH
WID = GROUP * TOK
CHUNKS = 4
ROWS = TOK // CHUNKS

NEG_FILL = -1e30
EPSILON = 1e-05
EXP_SCALE = DH ** (-0.5) * math.log2(math.e)

NT = (((1,), (1,)), ((), ()))


def kernel(
    x_hbm, q_hbm, k_hbm, w_hbm, gain_ref, dy_hbm,
    passed_hbm, wout_ref, gout_ref,
    xfull, dyfull, qb, dyb, xb, kall, wall,
    irms, gtile, gall, mref, lref, term,
    vsend, vrecv, vgs, vgall,
    normt, wsend, wrecv, usend, urecv, outb, gsend, grecv, gpart,
    loc, ys, yr, kxs, kxr, wxs, wxr, vs, vr, ws, wr, us, ur, ps, pr, gs, gr, hs, hr,
):
    sec = lax.axis_index("section")
    fsdp = lax.axis_index("fsdp")
    dp = lax.axis_index("dp")
    n_sec = lax.axis_size("section")
    row = fsdp // NZ
    z = lax.rem(fsdp, NZ)
    c = row * 2 + dp

    def at(cy, cz):
        return (sec, (cy // 2) * NZ + cz, lax.rem(cy, 2))

    def ypeer(o):
        return lax.rem(c + o, NY)

    def zoff(o):
        return lax.rem(z + (o + NZ), NZ)

    def lanes(start, size):
        return pl.ds(pl.multiple_of(start, 128), size)

    below = (lax.rem(sec + (n_sec - 1), n_sec), fsdp, dp)
    above = (lax.rem(sec + 1, n_sec), fsdp, dp)

    barrier = pltpu.get_barrier_semaphore()
    for o in range(1, NY):
        pl.semaphore_signal(barrier, inc=1, device_id=at(ypeer(o), z), device_id_type=MESH)
    for o in range(1, NZ):
        pl.semaphore_signal(barrier, inc=1, device_id=at(c, zoff(o)), device_id_type=MESH)
    pl.semaphore_signal(barrier, inc=1, device_id=below, device_id_type=MESH)
    pl.semaphore_signal(barrier, inc=1, device_id=above, device_id_type=MESH)

    sent = []

    def remote(src, dst, ssem, rsem, device):
        return pltpu.make_async_remote_copy(
            src_ref=src, dst_ref=dst, send_sem=ssem, recv_sem=rsem,
            device_id=device, device_id_type=MESH,
        )

    def send(*args):
        copy = remote(*args)
        copy.start()
        sent.append(copy)
        return copy

    def feature(part, piece):
        return lanes((part // 2) * (D // 2) + piece * 256 + lax.rem(part, 2) * 128, 128)

    x_local = pltpu.make_async_copy(x_hbm, xfull, loc.at[0])
    k_local = pltpu.make_async_copy(k_hbm.at[:, lanes(c * KC, KC)], kall.at[z, c], loc.at[1])
    q_local = pltpu.make_async_copy(q_hbm.at[:, lanes(c * QC, QC)], qb.at[c], loc.at[2])
    dyc_local = pltpu.make_async_copy(dy_hbm.at[:, lanes(c * QC, QC)], dyb.at[c], loc.at[3])
    w_local = pltpu.make_async_copy(w_hbm.at[lanes(dp * 128, 128), :], wall.at[z], loc.at[4])
    dy_local = pltpu.make_async_copy(dy_hbm, dyfull, loc.at[5])
    for copy in (k_local, w_local, x_local, q_local, dyc_local, dy_local):
        copy.start()

    half = jnp.where(dp == 0, gain_ref[:, 0:128].astype(F32), gain_ref[:, 128:256].astype(F32))
    gtile[...] = jnp.broadcast_to(half, (8, 128))

    pl.semaphore_wait(barrier, (NY - 1) + (NZ - 1) + 2)

    def k_send(o):
        pc = ypeer(o)
        return (k_hbm.at[:, lanes(pc * KC, KC)], kall.at[z, c], ys.at[0, o - 1], yr.at[0, o - 1], at(pc, z))

    def q_send(o):
        pc = ypeer(o)
        return (q_hbm.at[:, lanes(pc * QC, QC)], qb.at[c], ys.at[1, o - 1], yr.at[1, o - 1], at(pc, z))

    def dy_send(o):
        pc = ypeer(o)
        return (dy_hbm.at[:, lanes(pc * QC, QC)], dyb.at[c], ys.at[2, o - 1], yr.at[2, o - 1], at(pc, z))

    order = (2, 1, 3)
    k_recv = {o: send(*k_send(o)) for o in order}
    def ring_send(buf, step, way, halves, size, ssem, rsem):
        block = zoff(-step) if way == 0 else zoff(step)
        target = at(c, zoff(1) if way == 0 else zoff(-1))
        out = []
        for h in halves:
            ref = buf.at[block, pl.ds(h * size, size)]
            out.append(send(ref, ref, ssem.at[way, step, h], rsem.at[way, step, h], target))
        return out

    def ring_wait(buf, step, way, halves, size, ssem, rsem):
        block = zoff(-1 - step) if way == 0 else zoff(1 + step)
        for h in halves:
            ref = buf.at[block, pl.ds(h * size, size)]
            remote(ref, ref, ssem.at[way, step, h], rsem.at[way, step, h], at(c, zoff(1))).wait_recv()

    def halves_of(step, way):
        if step < 3:
            return (0, 1)
        return (0,) if way == 0 else (1,)

    def ag_send(which, step):
        buf, size, ssem, rsem = which
        for way in (0, 1):
            ring_send(buf, step, way, halves_of(step, way), size, ssem, rsem)

    def ag_wait(which, step):
        buf, size, ssem, rsem = which
        for way in (0, 1):
            ring_wait(buf, step, way, halves_of(step, way), size, ssem, rsem)

    kring = (kall, 2, kxs, kxr)
    wring = (wall, 64, wxs, wxr)

    w_local.wait()
    ag_send(wring, 0)
    q_recv = {o: send(*q_send(o)) for o in order}
    dy_recv = {o: send(*dy_send(o)) for o in order}
    for o in range(1, NZ):
        send(gtile, gall.at[z], gs.at[o - 1], gr.at[o - 1], at(c, zoff(o)))
    gall[z] = gtile[...]

    for o in order:
        k_recv[o].wait_recv()
    k_local.wait()
    ag_send(kring, 0)

    x_whole = {}
    for o in order:
        pc = ypeer(o)
        for piece in range(NZ):
            remote(
                x_hbm.at[:, feature(pc, piece)], xb.at[c, :, pl.ds(piece * 128, 128)],
                ys.at[3, o - 1], yr.at[3, o - 1], at(pc, z),
            ).start()
        x_whole[o] = remote(xb.at[c], xb.at[c], ys.at[3, o - 1], yr.at[3, o - 1], at(pc, z))
    x_local.wait()
    for piece in range(NZ):
        xb[c, :, piece * 128:(piece + 1) * 128] = xfull[:, feature(c, piece)]
    squares = jnp.zeros((TOK, 128), F32)
    for col in range(D // 128):
        v = xfull[:, col * 128:(col + 1) * 128].astype(F32)
        squares = squares + v * v
    rms = lax.rsqrt(jnp.sum(squares, axis=1, keepdims=True) * (1.0 / D) + EPSILON)
    irms[c] = jnp.broadcast_to(rms, (TOK, 128))
    r_recv = {
        o: send(irms.at[c], irms.at[c], ys.at[4, o - 1], yr.at[4, o - 1], at(ypeer(o), z)) for o in order
    }

    mref[...] = jnp.full_like(mref, NEG_FILL)
    lref[...] = jnp.zeros_like(lref)

    def stack(buf, src, g):
        return jnp.concatenate(
            [buf[src, :, lanes(g * WID + h * DH, DH)] for h in range(GROUP)], axis=0
        )

    def scores(src, block, ksrc, g):
        k = kall[block, ksrc, :, lanes(g * DH, DH)]
        return lax.dot_general(k, stack(qb, src, g), NT, preferred_element_type=F32)

    def diagonal(s, open_all):
        key = lax.broadcasted_iota(jnp.int32, (TOK, WID), 0)
        tok = lax.rem(lax.broadcasted_iota(jnp.int32, (TOK, WID), 1), TOK)
        seen = key <= tok
        if open_all is not None:
            seen = seen | open_all
        return jnp.where(seen, s, NEG_FILL)

    def update(idx, s):
        s = s.reshape(TOK // 8, 8, WID)
        old = mref[idx]
        new = jnp.maximum(old, jnp.max(s, axis=0))
        p = jnp.exp2((s - new[None]) * EXP_SCALE)
        lref[idx] = lref[idx] * jnp.exp2((old - new) * EXP_SCALE) + jnp.sum(p, axis=0)
        mref[idx] = new

    def pass_one(block, own):
        def body(j, carry):
            d, g = j // GL, lax.rem(j, GL)
            update(4 + j, scores(2 + d, block, d, g))

            def lower():
                a = scores(2 + d, block, 2 + d, g)
                b = scores(d, block, d, g)
                if own:
                    a = diagonal(a, None)
                    b = diagonal(b, z == 0)
                update(4 + j, a)
                update(j, b)

            if own:
                lower()
            else:
                pl.when(block <= z)(lower)
            return carry

        lax.fori_loop(0, 2 * GL, body, 0)

    def finish_stats():
        for idx in range(8):
            m8 = mref[idx]
            m = jnp.max(m8, axis=0, keepdims=True)
            total = jnp.sum(lref[idx] * jnp.exp2((m8 - m) * EXP_SCALE), axis=0, keepdims=True)
            mref[idx] = jnp.broadcast_to(m * EXP_SCALE + jnp.log(total) * math.log2(math.e), (8, WID))

    def weights(idx, s):
        p = jnp.exp2(s.reshape(TOK // 8, 8, WID) * EXP_SCALE - mref[idx][None])
        return p.reshape(TOK, WID).astype(BF16)

    def pass_two(slot, block, own):
        def body(j, carry):
            d, g = j // GL, lax.rem(j, GL)
            dy1 = stack(dyb, 2 + d, g)
            p = weights(4 + j, scores(2 + d, block, d, g))
            upper = jnp.dot(p, dy1, preferred_element_type=F32)

            def lower():
                a = scores(2 + d, block, 2 + d, g)
                b = scores(d, block, d, g)
                if own:
                    a = diagonal(a, None)
                    b = diagonal(b, z == 0)
                pa = weights(4 + j, a)
                pb = weights(j, b)
                term[slot, 2 + d, :, lanes(g * DH, DH)] = jnp.dot(pa, dy1, preferred_element_type=F32)
                term[slot, d, :, lanes(g * DH, DH)] = upper + jnp.dot(
                    pb, stack(dyb, d, g), preferred_element_type=F32
                )

            def upper_only():
                term[slot, 2 + d, :, lanes(g * DH, DH)] = jnp.zeros((TOK, DH), F32)
                term[slot, d, :, lanes(g * DH, DH)] = upper

            if own:
                lower()
            else:
                pl.when(block <= z)(lower)
                pl.when(block > z)(upper_only)
            return carry

        lax.fori_loop(0, 2 * GL, body, 0)

    ag_wait(kring, 0)
    ag_send(kring, 1)
    ag_wait(kring, 1)
    ag_send(kring, 2)
    for o in order:
        q_recv[o].wait_recv()
    q_local.wait()
    pass_one(z, True)
    pass_one(zoff(-1), False)
    pass_one(zoff(1), False)
    ag_wait(kring, 2)
    ag_send(kring, 3)
    ag_wait(wring, 0)
    ag_send(wring, 1)
    pass_one(zoff(-2), False)
    pass_one(zoff(2), False)
    pass_one(zoff(-3), False)
    pass_one(zoff(3), False)
    ag_wait(kring, 3)
    pass_one(zoff(4), False)
    finish_stats()

    for o in order:
        dy_recv[o].wait_recv()
    dyc_local.wait()

    def rs_args(sbuf, rbuf, ssem, rsem, step, way, h, size):
        return (
            sbuf.at[way, step, pl.ds(h * size, size)], rbuf.at[way, step, pl.ds(h * size, size)],
            ssem.at[way, step, h], rsem.at[way, step, h], at(c, zoff(1) if way == 0 else zoff(-1)),
        )

    def started(step, way, h):
        return step > 0 or h == way

    def rs_step(own_of, sbuf, rbuf, ssem, rsem, step, size):
        for way in (0, 1):
            for h in (0, 1):
                if not started(step, way, h):
                    continue
                part = pl.ds(h * size, size)
                value = own_of(way, part)
                if step > 0 and started(step - 1, way, h):
                    remote(*rs_args(sbuf, rbuf, ssem, rsem, step - 1, way, h, size)).wait_recv()
                    value = value + rbuf[way, step - 1, part].astype(F32)
                sbuf[way, step, part] = value.astype(BF16)
                send(*rs_args(sbuf, rbuf, ssem, rsem, step, way, h, size))

    def rs_last(own_of, sbuf, rbuf, ssem, rsem, h, size):
        part = pl.ds(h * size, size)
        value = own_of(0, part)
        for way in (0, 1):
            remote(*rs_args(sbuf, rbuf, ssem, rsem, 3, way, h, size)).wait_recv()
            value = value + rbuf[way, 3, part].astype(F32)
        return value

    def term_of(way, part):
        return term[way, part]

    pass_two(0, zoff(4), False)
    rs_step(lambda way, part: term[0, part], vsend, vrecv, vs, vr, 0, 2)
    for step in (1, 2, 3):
        pass_two(0, zoff(4 - step), False)
        pass_two(1, zoff(step - 4), False)
        rs_step(term_of, vsend, vrecv, vs, vr, step, 2)
        if step == 2:
            for o in order:
                x_whole[o].wait_recv()
                r_recv[o].wait_recv()
            for o in range(1, NZ):
                src = zoff(-o)
                remote(gtile, gall.at[src], gs.at[o - 1], gr.at[o - 1], at(c, src)).wait_recv()

            def norm_body(piece, carry):
                gain_row = gall[piece, 0:1, :]
                for src in range(NY):
                    xhat = xb[src, :, lanes(piece * 128, 128)].astype(F32) * irms[src]
                    normed = (xhat * gain_row).astype(BF16)
                    normt[piece, :, src * TOK:(src + 1) * TOK] = normed.T
                return carry

            lax.fori_loop(0, NZ, norm_body, 0)
    pass_two(0, z, True)
    for h in (0, 1):
        vgs[h * 2:h * 2 + 2] = rs_last(term_of, vsend, vrecv, vs, vr, h, 2).astype(BF16)
    v_recv = {
        o: send(vgs, vgall.at[:, :, lanes(c * KC, KC)], ys.at[5, o - 1], yr.at[5, o - 1], at(ypeer(o), z))
        for o in order
    }
    vgall[:, :, lanes(c * KC, KC)] = vgs[...]
    ag_wait(wring, 1)
    ag_send(wring, 2)
    ag_wait(wring, 2)
    ag_send(wring, 3)
    for o in order:
        src = ypeer(NY - o)
        remote(vgs, vgall.at[:, :, lanes(src * KC, KC)], ys.at[5, o - 1], yr.at[5, o - 1], at(src, z)).wait_recv()

    def weight_part(slot, piece):
        vg = vgall[...].reshape(NY * TOK, KV)
        term2 = jnp.dot(normt[piece], vg, preferred_element_type=F32)
        return term2

    def wpiece(step):
        low = weight_part(0, zoff(4 - step))
        high = low if step == 0 else weight_part(1, zoff(step - 4))
        return lambda way, part: (low, high)[way][part.start:part.start + part.size]

    rs_step(wpiece(0), wsend, wrecv, ws, wr, 0, 64)

    ag_wait(wring, 3)
    gain_wide = jnp.concatenate([gall[i, 0:1, :] for i in range(NZ)], axis=1)
    gpart[...] = jnp.zeros_like(gpart)
    weight_all = wall[...].reshape(NZ * 128, KV)

    for o in (2, 1, 3, 0):
        src = ypeer(o)
        ng = lax.dot_general(vgall[src], weight_all, NT, preferred_element_type=F32)
        usend[src] = (ng * gain_wide).astype(BF16)
        rr = irms[src]
        for piece in range(NZ):
            cols = slice(piece * 128, (piece + 1) * 128)
            prod = ng[:, cols] * (xb[src, :, cols].astype(F32) * rr)
            gpart[:, cols] += jnp.sum(prod.reshape(TOK // 8, 8, 128), axis=0)
    for t in range(CHUNKS):
        part = pl.ds(t * ROWS, ROWS)
        for o in order:
            src = ypeer(o)
            send(usend.at[src, part], urecv.at[c, part], us.at[o - 1, t], ur.at[o - 1, t], at(src, z))
    for piece in range(NZ):
        total = jnp.sum(gpart[:, piece * 128:(piece + 1) * 128], axis=0, keepdims=True)
        gsend[piece] = jnp.broadcast_to(total, (8, 128))
    for o in range(1, NZ):
        send(gsend.at[zoff(o)], grecv.at[o], hs.at[o - 1], hr.at[o - 1], at(c, zoff(o)))
    dy_local.wait()

    def finalize(t):
        part = pl.ds(t * ROWS, ROWS)
        for o in order:
            src = ypeer(NY - o)
            remote(
                usend.at[src, part], urecv.at[src, part], us.at[o - 1, t], ur.at[o - 1, t], at(src, z)
            ).wait_recv()
        urecv[c, part] = usend[c, part]
        rr = irms[c, part]
        acc = jnp.zeros((ROWS, 128), F32)
        for src in range(NY):
            for piece in range(NZ):
                base = (src // 2) * (D // 2) + piece * 256 + (src % 2) * 128
                xhat = xfull[part, base:base + 128].astype(F32) * rr
                acc = acc + urecv[src, part, piece * 128:(piece + 1) * 128].astype(F32) * xhat
        m = jnp.sum(acc, axis=1, keepdims=True) * (1.0 / D)
        for src in range(NY):
            for piece in range(NZ):
                base = (src // 2) * (D // 2) + piece * 256 + (src % 2) * 128
                xhat = xfull[part, base:base + 128].astype(F32) * rr
                u = urecv[src, part, piece * 128:(piece + 1) * 128].astype(F32)
                grad = dyfull[part, base:base + 128].astype(F32) + rr * (u - xhat * m)
                outb[part, base:base + 128] = grad.astype(BF16)
        send(outb.at[part], passed_hbm.at[part], ps.at[t], pr.at[t], below)

    rs_step(wpiece(1), wsend, wrecv, ws, wr, 1, 64)
    finalize(0)
    finalize(1)
    rs_step(wpiece(2), wsend, wrecv, ws, wr, 2, 64)
    finalize(2)
    finalize(3)
    rs_step(wpiece(3), wsend, wrecv, ws, wr, 3, 64)
    gtotal = gsend[z]
    for o in range(1, NZ):
        remote(gsend.at[z], grecv.at[o], hs.at[o - 1], hr.at[o - 1], at(c, zoff(o))).wait_recv()
        gtotal = gtotal + grecv[o]
    gout_ref[...] = gtotal[0:1]
    last = weight_part(0, z)
    for h in (0, 1):
        value = rs_last(lambda way, part: last[part.start:part.start + part.size], wsend, wrecv, ws, wr, h, 64)
        wout_ref[h * 64:(h + 1) * 64] = value.astype(BF16)
    for t in range(CHUNKS):
        part = pl.ds(t * ROWS, ROWS)
        remote(outb.at[part], passed_hbm.at[part], ps.at[t], pr.at[t], below).wait_recv()
    for o in order:
        x_whole[o].wait_send()
    for copy in sent:
        copy.wait_send()


def per_device(section_inputs, queries, keys, w_value, gain, section_grads_in):
    dma = pltpu.SemaphoreType.DMA
    vmem = pltpu.VMEM
    any_space = pl.BlockSpec(memory_space=pl.ANY)
    in_vmem = pl.BlockSpec(memory_space=pltpu.VMEM)
    passed, weight, gains = pl.pallas_call(
        kernel,
        out_shape=(
            jax.ShapeDtypeStruct((TOK, D), BF16),
            jax.ShapeDtypeStruct((TOK, KV), BF16),
            jax.ShapeDtypeStruct((1, 128), F32),
        ),
        in_specs=[any_space, any_space, any_space, any_space, in_vmem, any_space],
        out_specs=(any_space, in_vmem, in_vmem),
        scratch_shapes=[
            vmem((TOK, D), BF16),
            vmem((TOK, D), BF16),
            vmem((NY, TOK, QC), BF16),
            vmem((NY, TOK, QC), BF16),
            vmem((NY, TOK, QC), BF16),
            vmem((NZ, NY, TOK, KC), BF16),
            vmem((NZ, 128, KV), BF16),
            vmem((NY, TOK, 128), F32),
            vmem((8, 128), F32),
            vmem((NZ, 8, 128), F32),
            vmem((8, 8, WID), F32),
            vmem((8, 8, WID), F32),
            vmem((2, NY, TOK, KC), F32),
            vmem((2, 4, NY, TOK, KC), BF16),
            vmem((2, 4, NY, TOK, KC), BF16),
            vmem((NY, TOK, KC), BF16),
            vmem((NY, TOK, KV), BF16),
            vmem((NZ, 128, NY * TOK), BF16),
            vmem((2, 4, 128, KV), BF16),
            vmem((2, 4, 128, KV), BF16),
            vmem((NY, TOK, QC), BF16),
            vmem((NY, TOK, QC), BF16),
            vmem((TOK, D), BF16),
            vmem((NZ, 8, 128), F32),
            vmem((NZ, 8, 128), F32),
            vmem((8, QC), F32),
            dma((6,)),
            dma((6, 3)), dma((6, 3)),
            dma((2, 4, 2)), dma((2, 4, 2)),
            dma((2, 4, 2)), dma((2, 4, 2)),
            dma((2, 4, 2)), dma((2, 4, 2)),
            dma((2, 4, 2)), dma((2, 4, 2)),
            dma((3, CHUNKS)), dma((3, CHUNKS)),
            dma((CHUNKS,)), dma((CHUNKS,)),
            dma((NZ - 1,)), dma((NZ - 1,)),
            dma((NZ - 1,)), dma((NZ - 1,)),
        ],
        compiler_params=pltpu.CompilerParams(
            collective_id=0, has_side_effects=True, vmem_limit_bytes=60 * 1024 * 1024
        ),
        name="tick",
    )(section_inputs[0, 0], queries[0, 0], keys[0, 0], w_value[0], gain, section_grads_in[0, 0])
    return passed[None, None], weight[None], gains


def solution(mesh):
    return jax.shard_map(
        per_device,
        mesh=mesh,
        in_specs=(
            P("section", "dp", "fsdp", None),
            P("section", "dp", "fsdp", None),
            P("section", "dp", "fsdp", None),
            P("section", "fsdp", None),
            P("section", "fsdp"),
            P("section", "dp", "fsdp", None),
        ),
        out_specs=(
            P("section", "dp", "fsdp", None),
            P("section", ("fsdp", "dp"), None),
            P("section", ("fsdp", "dp")),
        ),
        check_vma=False,
    )
```

time: 727 us -> 130 us (0.18)
  waiting for transfers between devices: 532 us -> 0 us
  Pallas kernels: 0 us -> 126 us
  blocking collectives: 92.1 us -> 0 us
  matrix products: 66.8 us -> 0 us
  between operations: 14.5 us -> 0.65 us
  local copies, waits for them, and re-layouts: 13 us -> 3.55 us
    all_gather x2 -> x0, waiting for transfers between devices: 236 us -> none  [the longest x1 132 us: per_device(): lax.all_gather(w_value[0], 'fsdp', axis=0, tiled=True)]
    unnamed x5 -> x0, waiting for transfers between devices: 177 us -> none
    pallas_call x0 -> x1, Pallas kernels: none -> 126 us  [per_device(): pl.pallas_call(kernel, out_shape=(jax.ShapeDtypeStruct((TOK, D), BF16), j...]
    reduce_scatter x1 -> x0, waiting for transfers between devices: 119 us -> none  [per_device(): lax.psum_scatter(weight_part.astype(jnp.bfloat16), ('fsdp', 'dp'), scatte...]
    unnamed x1 -> x0, blocking collectives: 62.6 us -> none
    dot_general x10 -> x0, matrix products: 44.4 us -> none  [the longest x8 31.2 us: group_values(): jnp.einsum('htk,thd->kd', attn_probs, grad_group, preferred_element_type=...]
    all_gather x1 -> x0, blocking collectives: 29.5 us -> none  [per_device(): lax.all_gather(gain[0], 'fsdp', axis=0, tiled=True)]
    sub x8 -> x0, matrix products: 22.5 us -> none  [group_values(): weights_exp = jnp.exp(scores - row_top)]
  transfers between devices with their start and end apart: 5 -> 0, of which waited for: 4 -> 0; matrix products, arithmetic and copies ran while one was open for 3% -> 0% of each run, Pallas kernels for 0% -> 0%
where the time goes in v1:
time: 130 us
  Pallas kernels  126 us (97%)
  local copies, waits for them, and re-layouts  3.55 us (3%)
    pallas_call x1, Pallas kernels, per_device(): pl.pallas_call(kernel, out_shape=(jax.ShapeDtypeStruct((TOK, D), BF16), j...  126 us
    unnamed x7, local copies, waits for them, and re-layouts  3.55 us

profile of v1, /device:TPU:1, one launch (start us, length us, event | category | flops | bytes accessed | tf_op | source)
XLA Modules:
  0.0 130.0 jit_solution(17979389606760360140)
XLA Ops:
  0.6 125.8 %tick.1 = (bf16[128,4096]{1,0:T(8,128)(2,1)}, bf16[128,1024]{1,0:T(8,128)(2,1)}, f32[1,128]{1,0:T(1,128)}) custom-call(bf16[128,4096]{1,0:T(8,128)(2,1)} %bitcast.7, bf16[128,4096]{1,0:T(8,128)(2,1)} %bitcast.8, bf16[128,1024]{1,0:T(8,128)(2,1)} %bitcast.12, bf16[256,1024]{1,0:T(8,128)(2,1)} %bitcast.11, bf16[1,256]{1,0:T(2,128)(2,1)} %gain_ref.1, ...), custom_call_target="tpu_custom_call" | custom-call | tf_op jit(solution)/shard_map/tick/pallas_call | solution.py:473
  126.5 0.0 copy-start
  126.5 2.3 %copy.12 = bf16[1,1,128,4096]{3,2,1,0:T(8,128)(2,1)} copy(bf16[1,1,128,4096]{3,2,1,0:T(8,128)(2,1)} %bitcast.10) | data formatting | bytes 2097152
  128.8 0.0 copy-done
  128.8 0.0 copy-start.1
  128.8 0.7 copy.13
  129.5 0.0 copy-done.1
  129.5 0.5 copy.14
Async XLA Ops:
  126.5 2.3 %copy-start = (bf16[128,1024]{1,0:T(8,128)(2,1)S(1)}, bf16[128,1024]{1,0:T(8,128)(2,1)}, u32[]{:S(2)}) copy-start(bf16[128,1024]{1,0:T(8,128)(2,1)} %get-tuple-element.7) | copy-start | bytes 786436
  128.8 0.7 copy-start.1

commit v2 on v1

v2 whole, which is shorter than its diff:
```python
import functools
import math

import jax
import jax.numpy as jnp
from jax import lax
from jax.experimental import pallas as pl
from jax.experimental.pallas import tpu as pltpu
from jax.sharding import PartitionSpec as P

MESH = pl.DeviceIdType.MESH
BF16, F32 = jnp.bfloat16, jnp.float32

NY = 4
NZ = 8
TOK = 128
D = 4096
KV = 1024
DH = 128
GROUP = 4
QC = D // NY
KC = KV // NY
GL = KC // DH
WID = GROUP * TOK
CHUNKS = 4
ROWS = TOK // CHUNKS

NEG_FILL = -1e30
EPSILON = 1e-05
EXP_SCALE = DH ** (-0.5) * math.log2(math.e)

NT = (((1,), (1,)), ((), ()))


def kernel(
    x_hbm, q_hbm, k_hbm, w_hbm, gain_ref, dy_hbm,
    passed_hbm, wout_ref, gout_ref,
    xfull, dyfull, qb, dyb, xb, kall, wall,
    irms, gtile, gall, mref, lref, term,
    vsend, vrecv, vgs, vgall,
    normt, wsend, wrecv, usend, urecv, outb, gsend, grecv, gpart,
    loc, ys, yr, kxs, kxr, wxs, wxr, vs, vr, ws, wr, us, ur, ps, pr, gs, gr, hs, hr,
):
    sec = lax.axis_index("section")
    fsdp = lax.axis_index("fsdp")
    dp = lax.axis_index("dp")
    n_sec = lax.axis_size("section")
    row = fsdp // NZ
    z = lax.rem(fsdp, NZ)
    c = row * 2 + dp

    def at(cy, cz):
        return (sec, (cy // 2) * NZ + cz, lax.rem(cy, 2))

    def ypeer(o):
        return lax.rem(c + o, NY)

    def zoff(o):
        return lax.rem(z + (o + NZ), NZ)

    def lanes(start, size):
        return pl.ds(pl.multiple_of(start, 128), size)

    below = (lax.rem(sec + (n_sec - 1), n_sec), fsdp, dp)
    above = (lax.rem(sec + 1, n_sec), fsdp, dp)

    barrier = pltpu.get_barrier_semaphore()
    for o in range(1, NY):
        pl.semaphore_signal(barrier, inc=1, device_id=at(ypeer(o), z), device_id_type=MESH)
    for o in (1, -1):
        pl.semaphore_signal(barrier, inc=1, device_id=at(c, zoff(o)), device_id_type=MESH)
    pl.semaphore_signal(barrier, inc=1, device_id=below, device_id_type=MESH)
    pl.semaphore_signal(barrier, inc=1, device_id=above, device_id_type=MESH)

    sent = []

    def remote(src, dst, ssem, rsem, device):
        return pltpu.make_async_remote_copy(
            src_ref=src, dst_ref=dst, send_sem=ssem, recv_sem=rsem,
            device_id=device, device_id_type=MESH,
        )

    def send(*args):
        copy = remote(*args)
        copy.start()
        sent.append(copy)
        return copy

    def feature(part, piece):
        return lanes((part // 2) * (D // 2) + piece * 256 + lax.rem(part, 2) * 128, 128)

    x_local = pltpu.make_async_copy(x_hbm, xfull, loc.at[0])
    k_local = pltpu.make_async_copy(k_hbm.at[:, lanes(c * KC, KC)], kall.at[z, c], loc.at[1])
    q_local = pltpu.make_async_copy(q_hbm.at[:, lanes(c * QC, QC)], qb.at[c], loc.at[2])
    dyc_local = pltpu.make_async_copy(dy_hbm.at[:, lanes(c * QC, QC)], dyb.at[c], loc.at[3])
    w_local = pltpu.make_async_copy(w_hbm.at[lanes(dp * 128, 128), :], wall.at[z], loc.at[4])
    dy_local = pltpu.make_async_copy(dy_hbm, dyfull, loc.at[5])
    for copy in (k_local, w_local, x_local, q_local, dyc_local, dy_local):
        copy.start()

    half = jnp.where(dp == 0, gain_ref[:, 0:128].astype(F32), gain_ref[:, 128:256].astype(F32))
    gtile[...] = jnp.broadcast_to(half, (8, 128))

    pl.semaphore_wait(barrier, (NY - 1) + 2 + 2)

    def k_send(o):
        pc = ypeer(o)
        return (k_hbm.at[:, lanes(pc * KC, KC)], kall.at[z, c], ys.at[0, o - 1], yr.at[0, o - 1], at(pc, z))

    def q_send(o):
        pc = ypeer(o)
        return (q_hbm.at[:, lanes(pc * QC, QC)], qb.at[c], ys.at[1, o - 1], yr.at[1, o - 1], at(pc, z))

    def dy_send(o):
        pc = ypeer(o)
        return (dy_hbm.at[:, lanes(pc * QC, QC)], dyb.at[c], ys.at[2, o - 1], yr.at[2, o - 1], at(pc, z))

    order = (2, 1, 3)
    k_recv = {o: send(*k_send(o)) for o in order}
    def ring_args(ring, step, way, part, block):
        ref_of, _, ssem, rsem = ring
        ref = ref_of(block, part)
        target = at(c, zoff(1) if way == 0 else zoff(-1))
        return (ref, ref, ssem.at[way, step, part], rsem.at[way, step, part], target)

    def steps_of(way, part):
        return 4 if way == part % 2 else 3

    def ring_open(ring, part):
        for way in (0, 1):
            send(*ring_args(ring, 0, way, part, z))

    def ring_pass(ring, step):
        for part in range(ring[1]):
            for way in (0, 1):
                if step < steps_of(way, part):
                    block = zoff(-1 - step) if way == 0 else zoff(1 + step)
                    remote(*ring_args(ring, step, way, part, block)).wait_recv()
                    if step + 1 < steps_of(way, part):
                        send(*ring_args(ring, step + 1, way, part, block))

    around = (0, 1, 3, 2)

    def k_part(block, part):
        return kall.at[block, ypeer(NY - around[part])]

    def w_part(block, part):
        return wall.at[block, pl.ds(part * 64, 64)]

    def g_part(block, part):
        return gall.at[block]

    kring = (k_part, 4, kxs, kxr)
    wring = (w_part, 2, wxs, wxr)
    gring = (g_part, 1, gs, gr)

    k_local.wait()
    ring_open(kring, 0)
    w_local.wait()
    ring_open(wring, 0)
    q_recv = {o: send(*q_send(o)) for o in order}
    dy_recv = {o: send(*dy_send(o)) for o in order}
    gall[z] = gtile[...]
    for part in (1, 2, 3):
        k_recv[around[part]].wait_recv()
        ring_open(kring, part)
    for way in (0, 1):
        target = at(c, zoff(1) if way == 0 else zoff(-1))
        send(gtile, gall.at[z], gs.at[way, 0, 0], gr.at[way, 0, 0], target)

    x_whole = {}
    for o in order:
        pc = ypeer(o)
        for piece in range(NZ):
            remote(
                x_hbm.at[:, feature(pc, piece)], xb.at[c, :, pl.ds(piece * 128, 128)],
                ys.at[3, o - 1], yr.at[3, o - 1], at(pc, z),
            ).start()
        x_whole[o] = remote(xb.at[c], xb.at[c], ys.at[3, o - 1], yr.at[3, o - 1], at(pc, z))
    x_local.wait()
    for piece in range(NZ):
        xb[c, :, piece * 128:(piece + 1) * 128] = xfull[:, feature(c, piece)]
    squares = jnp.zeros((TOK, 128), F32)
    for col in range(D // 128):
        v = xfull[:, col * 128:(col + 1) * 128].astype(F32)
        squares = squares + v * v
    rms = lax.rsqrt(jnp.sum(squares, axis=1, keepdims=True) * (1.0 / D) + EPSILON)
    irms[c] = jnp.broadcast_to(rms, (TOK, 128))
    r_recv = {
        o: send(irms.at[c], irms.at[c], ys.at[4, o - 1], yr.at[4, o - 1], at(ypeer(o), z)) for o in order
    }

    mref[...] = jnp.full_like(mref, NEG_FILL)
    lref[...] = jnp.zeros_like(lref)

    def head(buf, src, g, h):
        return buf[src, :, lanes(g * WID + h * DH, DH)]

    def key_rows(block, ksrc, g):
        return kall[block, ksrc, :, lanes(g * DH, DH)]

    def scores(k, src, g, h):
        return lax.dot_general(k, head(qb, src, g, h), NT, preferred_element_type=F32)

    def seen_of(open_all):
        key = lax.broadcasted_iota(jnp.int32, (TOK, TOK), 0)
        seen = key <= lax.broadcasted_iota(jnp.int32, (TOK, TOK), 1)
        return seen if open_all is None else seen | open_all

    def update(idx, h, s):
        cols = slice(h * TOK, (h + 1) * TOK)
        s = s.reshape(s.shape[0] // 8, 8, TOK)
        old = mref[idx, :, cols]
        new = jnp.maximum(old, jnp.max(s, axis=0))
        p = jnp.exp2((s - new[None]) * EXP_SCALE)
        lref[idx, :, cols] = lref[idx, :, cols] * jnp.exp2((old - new) * EXP_SCALE) + jnp.sum(p, axis=0)
        mref[idx, :, cols] = new

    def repeat(body):
        lax.fori_loop(0, 2 * GL, body, 0, unroll=2)

    def pass_one(block, own):
        def full(j, carry):
            d, g = j // GL, lax.rem(j, GL)
            k0, k1 = key_rows(block, d, g), key_rows(block, 2 + d, g)
            both = jnp.concatenate([k0, k1], axis=0)
            for h in range(GROUP):
                a = scores(both, 2 + d, g, h)
                b = scores(k0, d, g, h)
                if own:
                    low = jnp.where(seen_of(None), a[TOK:], NEG_FILL)
                    a = jnp.concatenate([a[:TOK], low], axis=0)
                    b = jnp.where(seen_of(z == 0), b, NEG_FILL)
                update(4 + j, h, a)
                update(j, h, b)
            return carry

        def light(j, carry):
            d, g = j // GL, lax.rem(j, GL)
            k0 = key_rows(block, d, g)
            for h in range(GROUP):
                update(4 + j, h, scores(k0, 2 + d, g, h))
            return carry

        if own:
            repeat(full)
        else:
            pl.when(block <= z)(lambda: repeat(full))
            pl.when(block > z)(lambda: repeat(light))

    def finish_stats():
        for idx in range(8):
            m8 = mref[idx]
            m = jnp.max(m8, axis=0, keepdims=True)
            total = jnp.sum(lref[idx] * jnp.exp2((m8 - m) * EXP_SCALE), axis=0, keepdims=True)
            mref[idx] = jnp.broadcast_to(m * EXP_SCALE + jnp.log(total) * math.log2(math.e), (8, WID))

    def weights(idx, h, s):
        cols = slice(h * TOK, (h + 1) * TOK)
        p = jnp.exp2(s.reshape(s.shape[0] // 8, 8, TOK) * EXP_SCALE - mref[idx, :, cols][None])
        return p.reshape(s.shape).astype(BF16)

    def cotangents(src, g):
        return jnp.concatenate([head(dyb, src, g, h) for h in range(GROUP)], axis=0)

    def pass_two(slot, block, own):
        def full(j, carry):
            d, g = j // GL, lax.rem(j, GL)
            k0, k1 = key_rows(block, d, g), key_rows(block, 2 + d, g)
            both = jnp.concatenate([k0, k1], axis=0)
            pa, pb = [], []
            for h in range(GROUP):
                a = scores(both, 2 + d, g, h)
                b = scores(k0, d, g, h)
                if own:
                    low = jnp.where(seen_of(None), a[TOK:], NEG_FILL)
                    a = jnp.concatenate([a[:TOK], low], axis=0)
                    b = jnp.where(seen_of(z == 0), b, NEG_FILL)
                pa.append(weights(4 + j, h, a))
                pb.append(weights(j, h, b))
            upper = jnp.dot(jnp.concatenate(pa, axis=1), cotangents(2 + d, g), preferred_element_type=F32)
            lower = jnp.dot(jnp.concatenate(pb, axis=1), cotangents(d, g), preferred_element_type=F32)
            term[slot, d, :, lanes(g * DH, DH)] = upper[:TOK] + lower
            term[slot, 2 + d, :, lanes(g * DH, DH)] = upper[TOK:]
            return carry

        def light(j, carry):
            d, g = j // GL, lax.rem(j, GL)
            k0 = key_rows(block, d, g)
            pa = [weights(4 + j, h, scores(k0, 2 + d, g, h)) for h in range(GROUP)]
            term[slot, d, :, lanes(g * DH, DH)] = jnp.dot(
                jnp.concatenate(pa, axis=1), cotangents(2 + d, g), preferred_element_type=F32
            )
            term[slot, 2 + d, :, lanes(g * DH, DH)] = jnp.zeros((TOK, DH), F32)
            return carry

        if own:
            repeat(full)
        else:
            pl.when(block <= z)(lambda: repeat(full))
            pl.when(block > z)(lambda: repeat(light))

    ring_pass(kring, 0)
    ring_pass(gring, 0)
    ring_pass(kring, 1)
    for o in order:
        q_recv[o].wait_recv()
    q_local.wait()
    pass_one(z, True)
    pass_one(zoff(-1), False)
    ring_pass(kring, 2)
    ring_pass(gring, 1)
    ring_open(wring, 1)
    pass_one(zoff(1), False)
    pass_one(zoff(-2), False)
    ring_pass(kring, 3)
    ring_pass(wring, 0)
    pass_one(zoff(2), False)
    pass_one(zoff(-3), False)
    pass_one(zoff(3), False)
    pass_one(zoff(4), False)
    finish_stats()

    for o in order:
        dy_recv[o].wait_recv()
    dyc_local.wait()

    def rs_args(sbuf, rbuf, ssem, rsem, step, way, h, size):
        return (
            sbuf.at[way, step, pl.ds(h * size, size)], rbuf.at[way, step, pl.ds(h * size, size)],
            ssem.at[way, step, h], rsem.at[way, step, h], at(c, zoff(1) if way == 0 else zoff(-1)),
        )

    def started(step, way, h):
        return step > 0 or h == way

    def rs_step(own_of, sbuf, rbuf, ssem, rsem, step, size):
        for way, h in ((0, 1), (1, 0), (0, 0), (1, 1)):
            if not started(step, way, h):
                continue
            part = pl.ds(h * size, size)
            value = own_of(way, part)
            if step > 0 and started(step - 1, way, h):
                remote(*rs_args(sbuf, rbuf, ssem, rsem, step - 1, way, h, size)).wait_recv()
                value = value + rbuf[way, step - 1, part].astype(F32)
            sbuf[way, step, part] = value.astype(BF16)
            send(*rs_args(sbuf, rbuf, ssem, rsem, step, way, h, size))

    def rs_last(own_of, sbuf, rbuf, ssem, rsem, h, size):
        part = pl.ds(h * size, size)
        value = own_of(0, part)
        for way in (0, 1):
            remote(*rs_args(sbuf, rbuf, ssem, rsem, 3, way, h, size)).wait_recv()
            value = value + rbuf[way, 3, part].astype(F32)
        return value

    def term_of(way, part):
        return term[way, part]

    pass_two(0, zoff(4), False)
    rs_step(lambda way, part: term[0, part], vsend, vrecv, vs, vr, 0, 2)
    for step in (1, 2, 3):
        pass_two(0, zoff(4 - step), False)
        pass_two(1, zoff(step - 4), False)
        rs_step(term_of, vsend, vrecv, vs, vr, step, 2)
        if step < 3:
            ring_pass(wring, step)
        if step == 2:
            for o in order:
                x_whole[o].wait_recv()
                r_recv[o].wait_recv()
            ring_pass(gring, 2)
            ring_pass(gring, 3)

            def norm_body(piece, carry):
                gain_row = gall[piece, 0:1, :]
                for src in range(NY):
                    xhat = xb[src, :, lanes(piece * 128, 128)].astype(F32) * irms[src]
                    normed = (xhat * gain_row).astype(BF16)
                    normt[piece, :, src * TOK:(src + 1) * TOK] = normed.T
                return carry

            lax.fori_loop(0, NZ, norm_body, 0)
    pass_two(0, z, True)
    def v_args(h, o, src):
        rows = pl.ds(2 * h, 2)
        return (
            vgs.at[rows], vgall.at[rows, :, lanes(src * KC, KC)],
            ys.at[5 + h, o - 1], yr.at[5 + h, o - 1], at(ypeer(o), z),
        )

    def v_wait(h, o):
        remote(*v_args(h, o, ypeer(NY - o))).wait_recv()

    for h in (0, 1):
        half = rs_last(term_of, vsend, vrecv, vs, vr, h, 2).astype(BF16)
        vgs[2 * h:2 * h + 2] = half
        for o in order:
            send(*v_args(h, o, c))
        vgall[2 * h:2 * h + 2, :, lanes(c * KC, KC)] = half

    def weight_part(piece, q):
        cols = lanes(ypeer(NY - around[q]) * KC, KC)
        return jnp.dot(normt[piece], vgall[:, :, cols].reshape(NY * TOK, KC), preferred_element_type=F32)

    def w_args(step, way, q):
        return (
            wsend.at[way, step, q], wrecv.at[way, step, q], ws.at[way, step, q], wr.at[way, step, q],
            at(c, zoff(1) if way == 0 else zoff(-1)),
        )

    def w_step(q, step):
        for way in (1 - q % 2, q % 2):
            first = 0 if way == q % 2 else 1
            if step < first:
                continue
            value = weight_part(zoff(4 - step) if way == 0 else zoff(step - 4), q)
            if step > first:
                remote(*w_args(step - 1, way, q)).wait_recv()
                value = value + wrecv[way, step - 1, q].astype(F32)
            wsend[way, step, q] = value.astype(BF16)
            send(*w_args(step, way, q))

    def w_last(q):
        value = weight_part(z, q)
        for way in (0, 1):
            remote(*w_args(3, way, q)).wait_recv()
            value = value + wrecv[way, 3, q].astype(F32)
        wout_ref[:, lanes(ypeer(NY - around[q]) * KC, KC)] = value.astype(BF16)

    def g_args(step, way):
        return (
            gsend.at[way, step], grecv.at[way, step], hs.at[way, step], hr.at[way, step],
            at(c, zoff(1) if way == 0 else zoff(-1)),
        )

    def g_own(piece):
        return gpart[piece]

    def g_step(step):
        for way in (1, 0):
            if step < way:
                continue
            value = g_own(zoff(4 - step) if way == 0 else zoff(step - 4))
            if step > way:
                remote(*g_args(step - 1, way)).wait_recv()
                value = value + grecv[way, step - 1]
            gsend[way, step] = value
            send(*g_args(step, way))

    gain_wide = jnp.concatenate([gall[i, 0:1, :] for i in range(NZ)], axis=1)

    def u_args(src, t):
        part = pl.ds(t * ROWS, ROWS)
        o = lax.rem(src - c + NY, NY)
        return (usend.at[src, part], urecv.at[c, part], us.at[src, t], ur.at[o, t], at(src, z))

    def u_step(src):
        weight_all = wall[...].reshape(NZ * 128, KV)
        ng = lax.dot_general(vgall[src], weight_all, NT, preferred_element_type=F32)
        usend[src] = (ng * gain_wide).astype(BF16)

        @pl.when(c != src)
        def _():
            for t in range(CHUNKS):
                remote(*u_args(src, t)).start()

        rr = irms[src]
        for piece in range(NZ):
            cols = slice(piece * 128, (piece + 1) * 128)
            prod = ng[:, cols] * (xb[src, :, cols].astype(F32) * rr)
            total = jnp.sum(prod.reshape(TOK // 8, 8, 128), axis=0)
            gpart[piece] = total if src == 0 else gpart[piece] + total

    w_step(0, 0)
    ring_pass(wring, 3)
    w_step(0, 1)
    for o in order:
        v_wait(0, o)
    u_step(0)
    u_step(1)
    w_step(0, 2)
    for q in (1, 2, 3):
        v_wait(1, around[q])
        w_step(q, 0)
    u_step(2)
    u_step(3)
    g_step(0)
    dy_local.wait()

    def finalize(t):
        part = pl.ds(t * ROWS, ROWS)
        for o in order:
            src = ypeer(NY - o)
            remote(
                usend.at[src, part], urecv.at[src, part], us.at[src, t], ur.at[o, t], at(src, z)
            ).wait_recv()
        urecv[c, part] = usend[c, part]
        rr = irms[c, part]
        acc = jnp.zeros((ROWS, 128), F32)
        for src in range(NY):
            for piece in range(NZ):
                base = (src // 2) * (D // 2) + piece * 256 + (src % 2) * 128
                xhat = xfull[part, base:base + 128].astype(F32) * rr
                acc = acc + urecv[src, part, piece * 128:(piece + 1) * 128].astype(F32) * xhat
        m = jnp.sum(acc, axis=1, keepdims=True) * (1.0 / D)
        for src in range(NY):
            for piece in range(NZ):
                base = (src // 2) * (D // 2) + piece * 256 + (src % 2) * 128
                xhat = xfull[part, base:base + 128].astype(F32) * rr
                u = urecv[src, part, piece * 128:(piece + 1) * 128].astype(F32)
                grad = dyfull[part, base:base + 128].astype(F32) + rr * (u - xhat * m)
                outb[part, base:base + 128] = grad.astype(BF16)
        send(outb.at[part], passed_hbm.at[part], ps.at[t], pr.at[t], below)

    w_step(0, 3)
    for q in (1, 2, 3):
        w_step(q, 1)
    g_step(1)
    for q in (1, 2, 3):
        w_step(q, 2)
    g_step(2)
    finalize(0)
    for q in (1, 2, 3):
        w_step(q, 3)
    g_step(3)
    finalize(1)
    finalize(2)
    finalize(3)
    gtotal = g_own(z)
    for way in (0, 1):
        remote(*g_args(3, way)).wait_recv()
        gtotal = gtotal + grecv[way, 3]
    gout_ref[...] = jnp.sum(gtotal, axis=0, keepdims=True)
    for q in range(NY):
        w_last(q)
    for t in range(CHUNKS):
        part = pl.ds(t * ROWS, ROWS)
        remote(outb.at[part], passed_hbm.at[part], ps.at[t], pr.at[t], below).wait_recv()
    for o in order:
        x_whole[o].wait_send()
    for copy in sent:
        copy.wait_send()
    for src in range(NY):
        @pl.when(c != src)
        def _():
            for t in range(CHUNKS):
                remote(*u_args(src, t)).wait_send()


def per_device(section_inputs, queries, keys, w_value, gain, section_grads_in):
    dma = pltpu.SemaphoreType.DMA
    vmem = pltpu.VMEM
    any_space = pl.BlockSpec(memory_space=pl.ANY)
    in_vmem = pl.BlockSpec(memory_space=pltpu.VMEM)
    passed, weight, gains = pl.pallas_call(
        kernel,
        out_shape=(
            pltpu.VMEM((TOK, D), BF16),
            pltpu.VMEM((TOK, KV), BF16),
            pltpu.VMEM((1, 128), F32),
        ),
        in_specs=[any_space, any_space, any_space, any_space, in_vmem, any_space],
        out_specs=(in_vmem, in_vmem, in_vmem),
        scratch_shapes=[
            vmem((TOK, D), BF16),
            vmem((TOK, D), BF16),
            vmem((NY, TOK, QC), BF16),
            vmem((NY, TOK, QC), BF16),
            vmem((NY, TOK, QC), BF16),
            vmem((NZ, NY, TOK, KC), BF16),
            vmem((NZ, 128, KV), BF16),
            vmem((NY, TOK, 128), F32),
            vmem((8, 128), F32),
            vmem((NZ, 8, 128), F32),
            vmem((8, 8, WID), F32),
            vmem((8, 8, WID), F32),
            vmem((2, NY, TOK, KC), F32),
            vmem((2, 4, NY, TOK, KC), BF16),
            vmem((2, 4, NY, TOK, KC), BF16),
            vmem((NY, TOK, KC), BF16),
            vmem((NY, TOK, KV), BF16),
            vmem((NZ, 128, NY * TOK), BF16),
            vmem((2, 4, NY, 128, KC), BF16),
            vmem((2, 4, NY, 128, KC), BF16),
            vmem((NY, TOK, QC), BF16),
            vmem((NY, TOK, QC), BF16),
            vmem((TOK, D), BF16),
            vmem((2, 4, 8, 128), F32),
            vmem((2, 4, 8, 128), F32),
            vmem((NZ, 8, 128), F32),
            dma((6,)),
            dma((7, 3)), dma((7, 3)),
            dma((2, 4, 4)), dma((2, 4, 4)),
            dma((2, 4, 2)), dma((2, 4, 2)),
            dma((2, 4, 2)), dma((2, 4, 2)),
            dma((2, 4, 4)), dma((2, 4, 4)),
            dma((NY, CHUNKS)), dma((NY, CHUNKS)),
            dma((CHUNKS,)), dma((CHUNKS,)),
            dma((2, 4, 1)), dma((2, 4, 1)),
            dma((2, 4)), dma((2, 4)),
        ],
        compiler_params=pltpu.CompilerParams(
            collective_id=0, has_side_effects=True, vmem_limit_bytes=60 * 1024 * 1024
        ),
        name="tick",
    )(section_inputs[0, 0], queries[0, 0], keys[0, 0], w_value[0], gain, section_grads_in[0, 0])
    return passed[None, None], weight[None], gains


def solution(mesh):
    return jax.shard_map(
        per_device,
        mesh=mesh,
        in_specs=(
            P("section", "dp", "fsdp", None),
            P("section", "dp", "fsdp", None),
            P("section", "dp", "fsdp", None),
            P("section", "fsdp", None),
            P("section", "fsdp"),
            P("section", "dp", "fsdp", None),
        ),
        out_specs=(
            P("section", "dp", "fsdp", None),
            P("section", ("fsdp", "dp"), None),
            P("section", ("fsdp", "dp")),
        ),
        check_vma=False,
    )
```

time: 130 us -> 123 us (0.946)
  Pallas kernels: 126 us -> 120 us
  local copies, waits for them, and re-layouts: 3.55 us -> 2.18 us
    pallas_call x1, Pallas kernels: 126 us -> 120 us  [per_device(): pl.pallas_call(kernel, out_shape=(pltpu.VMEM((TOK, D), BF16), pltpu.VMEM(...]
    unnamed x7 -> x3, local copies, waits for them, and re-layouts: 3.55 us -> 2.18 us
where the time goes in v2:
time: 123 us
  Pallas kernels  120 us (98%)
  local copies, waits for them, and re-layouts  2.18 us (2%)
    pallas_call x1, Pallas kernels, per_device(): pl.pallas_call(kernel, out_shape=(pltpu.VMEM((TOK, D), BF16), pltpu.VMEM(...  120 us

profile of v2, /device:TPU:1, one launch (start us, length us, event | category | flops | bytes accessed | tf_op | source)
XLA Modules:
  0.0 122.5 jit_solution(11713935810137253709)
XLA Ops:
  0.6 119.7 %tick.1 = (bf16[128,4096]{1,0:T(8,128)(2,1)S(1)}, bf16[128,1024]{1,0:T(8,128)(2,1)S(1)}, f32[1,128]{1,0:T(1,128)S(1)}) custom-call(bf16[128,4096]{1,0:T(8,128)(2,1)} %bitcast.9, bf16[128,4096]{1,0:T(8,128)(2,1)} %bitcast.10, bf16[128,1024]{1,0:T(8,128)(2,1)} %bitcast.13, bf16[256,1024]{1,0:T(8,128)(2,1)} %bitcast.12, bf16[1,256]{1,0:T(2,128)(2,1)} %gain_ref.1, ...), custom_call_target="tpu_custom_call" | custom-call | tf_op jit(solution)/shard_map/tick/pallas_call | solution.py:556
  120.3 1.0 copy.12
  121.3 0.7 copy.13
  122.0 0.5 copy.14
